TPU v7x, 32 devices: a whole 2x2x4 slice. The times are simulated.
32 devices in a mesh: section: 2 (over core), dom: 16 (over z, y, x).
Axes of the slice: x: 2, y: 2, z: 4, core: 2. Of those that a mesh axis runs over, the one named last changes fastest.
Arguments:
- blocks: float32 [16, 32, 6, 128, 128], P('section', 'dom'), may hold values from -0.21875 to 0.21875
- column_index: int32 [16, 32, 6], P('section', 'dom'), may hold values from 0 to 31
- block_period: int32 [16, 32, 6], P('section', 'dom'), may hold values from 0 to 15, as said below
- cost_vector: float32 [16, 4096], P('section', 'dom'), may hold values from -6 to 6
- demand: float32 [16, 4096], P('section', 'dom'), may hold values from -12 to 12
- primal_start: float32 [16, 4096], P('section', 'dom'), may hold values from 0 to 2
- dual_start: float32 [16, 4096], P('section', 'dom'), may hold values from -3 to 3
- primal_weight: float32 [1], replicated, may hold values from 0.5 to 2
Outputs:
- primal_final: float32 [16, 4096], P('section', 'dom')
- dual_final: float32 [16, 4096], P('section', 'dom')
Inputs may be any that keep to these rules, and one draw needn't show every extreme that they name: block_period[p, r, k] is p or p - 1; it is p for k = 0 and for p = 0.
All inputs are finite; a program needn't handle non-finite values.
Results may differ from a plain program's by a relative error of at most 0.00011.
Values sent between devices are 32-bit elements; how exact they have to be, the bound alone decides.
A program may use at most 64 MiB of HBM per device.

v0:
```python
import jax
import jax.numpy as jnp
from jax import lax
from jax.sharding import PartitionSpec as P

step_scale = 0.4
epsilon = 1e-06


def passed_along(block, axis, distance):
    devices = range(lax.axis_size(axis))
    route = [(i - distance, i) for i in devices if i - distance in devices]
    return lax.ppermute(block, axis, route)


def slot_layout(column_index, block_period):
    periods_here = column_index.shape[0]
    local_period = jnp.arange(periods_here, dtype=jnp.int32)[:, None, None]
    global_period = lax.axis_index("section") * periods_here + local_period
    slot_index = local_period + block_period - global_period + 1
    return slot_index


def forward(blocks, column_index, slot_index, field):
    periods_here = field.shape[0]
    width_here = blocks.shape[-1]
    gathered = lax.all_gather(field, "dom", axis=1, tiled=True)
    carried = passed_along(gathered[-1:], "section", 1)
    stacked = jnp.concatenate([carried, gathered], axis=0)
    block_count = stacked.shape[1] // width_here
    picked = stacked.reshape(periods_here + 1, block_count, width_here)[slot_index, column_index]
    product = jnp.einsum("prkij,prkj->pri", blocks, picked, precision=lax.Precision.HIGHEST)
    return product.reshape(periods_here, -1)


def adjoint(blocks, column_index, slot_index, field):
    periods_here = field.shape[0]
    rows_here = blocks.shape[1]
    width_here = blocks.shape[-1]
    block_count = rows_here * lax.axis_size("dom")
    field_blocks = field.reshape(periods_here, rows_here, width_here)
    block_terms = jnp.einsum(
        "prkij,pri->prkj", blocks, field_blocks, precision=lax.Precision.HIGHEST
    )
    segment_ids = (slot_index * block_count + column_index).reshape(-1)
    dense_term = jax.ops.segment_sum(
        block_terms.reshape(-1, width_here),
        segment_ids,
        num_segments=(periods_here + 1) * block_count,
    )
    dense_term = dense_term.reshape(periods_here + 1, block_count * width_here)
    carried = passed_along(dense_term[:1], "section", -1)
    own_rows = dense_term[1:]
    merged = own_rows + jnp.concatenate([jnp.zeros_like(own_rows[:-1]), carried], axis=0)
    result = lax.psum_scatter(merged, "dom", scatter_dimension=1, tiled=True)
    return result


def on_device(
    blocks, column_index, block_period, cost_vector, demand, primal_start, dual_start, primal_weight
):
    slot_index = slot_layout(column_index, block_period)
    weight_now = primal_weight[0]
    tau_first = step_scale / weight_now
    sigma_first = step_scale * weight_now
    primal_one = jnp.maximum(
        0.0,
        primal_start
        - tau_first * (cost_vector - adjoint(blocks, column_index, slot_index, dual_start)),
    )
    dual_one = dual_start + sigma_first * (
        demand - forward(blocks, column_index, slot_index, 2.0 * primal_one - primal_start)
    )
    local_primal = jnp.sum((primal_one - primal_start) ** 2)
    local_dual = jnp.sum((dual_one - dual_start) ** 2)
    move_primal, move_dual = lax.psum((local_primal, local_dual), ("section", "dom"))
    weight_next = jnp.sqrt(weight_now * jnp.sqrt((move_dual + epsilon) / (move_primal + epsilon)))
    tau_second = step_scale / weight_next
    sigma_second = step_scale * weight_next
    primal_final = jnp.maximum(
        0.0,
        primal_one
        - tau_second * (cost_vector - adjoint(blocks, column_index, slot_index, dual_one)),
    )
    dual_final = dual_one + sigma_second * (
        demand - forward(blocks, column_index, slot_index, 2.0 * primal_final - primal_one)
    )
    return (primal_final, dual_final)


def solution(mesh):
    return jax.shard_map(
        on_device,
        mesh=mesh,
        in_specs=(
            P("section", "dom", None, None, None),
            P("section", "dom", None),
            P("section", "dom", None),
            P("section", "dom"),
            P("section", "dom"),
            P("section", "dom"),
            P("section", "dom"),
            P(),
        ),
        out_specs=(P("section", "dom"), P("section", "dom")),
        check_vma=False,
    )
```

profile of v0, /device:TPU:0, one launch (start us, length us, event | category | flops | bytes accessed | tf_op | source)
XLA Modules:
  0.0 288.4 jit_solution(15570511346201908841)
XLA Ops:
  7.2 0.7 fusion.14
  8.2 6.1 %fusion.10 = f32[8,2,1,6,128]{4,2,3,1,0:T(1,128)S(1)} fusion(f32[8,2,6,128,128]{4,3,2,1,0:T(8,128)} %param.8, f32[8,2,128,1,1]{2,0,1,3,4:T(8,128)} %bitcast.58), kind=kOutput, calls=%fused_computation.24 | convolution fusion | flops 18874368 | bytes 6348800 | tf_op jit(solution)/shard_map/prkij,pri->prkj/dot_general | solution.py:42
  14.3 0.9 scatter_custom_fusion
  15.2 1.3 collective-permute-start
  16.6 1.7 collective-permute-done
  18.3 0.7 pad_add_fusion.1
  19.8 78.9 %reduce-scatter.3.cloned.1.call-done = f32[8,256]{1,0:T(8,128)} async-done(((f32[8,4096]{1,0:T(8,128)}), f32[8,256]{1,0:T(8,128)}) %reduce-scatter.3.cloned.1.call-update) | async-done | bytes 8208 | tf_op jit(solution)/shard_map/reduce_scatter | solution.py:55
  98.7 1.3 multiply_reduce_fusion
  100.0 36.7 %all_gather.6 = f32[8,4096]{1,0:T(8,128)S(1)} all-gather(f32[8,256]{1,0:T(8,128)S(1)} %multiply_subtract_fusion.1), channel_id=1, replica_groups=mesh['section'=2,'dom'=16] {'dom'}, dimensions={1}, use_global_device_ids=true | all-gather | bytes 139264 | tf_op jit(solution)/shard_map/all_gather | solution.py:27
  136.7 1.3 collective-permute-start.1
  138.9 1.4 gather_fusion
  140.3 7.1 %fusion.18 = f32[8,2,1,128,1]{3,2,4,1,0:T(1,128)S(1)} fusion(f32[8,2,6,128,1]{3,4,2,1,0:T(1,128)S(1)} %bitcast.54, f32[8,2,6,128,128]{4,3,2,1,0:T(8,128)} %param.8), kind=kOutput, calls=%fused_computation.40 | convolution fusion | flops 18874368 | bytes 6348800 | tf_op jit(solution)/shard_map/prkij,prkj->pri/dot_general | solution.py:32
  147.4 0.7 multiply_reduce_fusion.1
  148.1 5.1 %fusion.8 = f32[8,2,1,6,128]{4,2,3,1,0:T(1,128)S(1)} fusion(f32[8,2,6,128,128]{4,3,2,1,0:T(8,128)} %param.8, f32[8,2,128,1,1]{2,0,1,3,4:T(8,128)S(1)} %bitcast.57), kind=kOutput, calls=%fused_computation.22 | convolution fusion | flops 18874368 | bytes 6348800 | tf_op jit(solution)/shard_map/prkij,pri->prkj/dot_general | solution.py:42
  153.2 0.9 scatter_custom_fusion.1
  154.1 1.3 collective-permute-start.2
  155.5 1.7 collective-permute-done.2
  157.9 37.2 %all-reduce.2 = (f32[]{:T(128)}, f32[]{:T(128)}) all-reduce(f32[]{:T(128)} %get-tuple-element.8, f32[]{:T(128)} %get-tuple-element.6), channel_id=1, replica_groups=mesh['section'=2,'dom'=16] {'section','dom'}, use_global_device_ids=true, to_apply=%region_3.0 | all-reduce | flops 2 | bytes 16 | tf_op jit(solution)/shard_map/psum | solution.py:76
  196.5 35.8 %reduce-scatter.5.cloned.1.call-done = f32[8,256]{1,0:T(8,128)} async-done(((f32[8,4096]{1,0:T(8,128)}), f32[8,256]{1,0:T(8,128)}) %reduce-scatter.5.cloned.1.call-update) | async-done | bytes 8208 | tf_op jit(solution)/shard_map/reduce_scatter | solution.py:55
  232.3 1.3 multiply_subtract_fusion
  233.6 36.6 %all_gather.7 = f32[8,4096]{1,0:T(8,128)S(1)} all-gather(f32[8,256]{1,0:T(8,128)S(1)} %get-tuple-element.4), channel_id=1, replica_groups=mesh['section'=2,'dom'=16] {'dom'}, dimensions={1}, use_global_device_ids=true | all-gather | bytes 139264 | tf_op jit(solution)/shard_map/all_gather | solution.py:27
  270.3 1.5 collective-permute-start.3
  272.5 1.4 gather_fusion.1
  273.9 7.1 %fusion.19 = f32[8,2,1,128,1]{3,2,4,1,0:T(1,128)S(1)} fusion(f32[8,2,6,128,1]{3,4,2,1,0:T(1,128)S(1)} %bitcast.53, f32[8,2,6,128,128]{4,3,2,1,0:T(8,128)} %param.8), kind=kOutput, calls=%fused_computation.41 | convolution fusion | flops 18874368 | bytes 6348800 | tf_op jit(solution)/shard_map/prkij,prkj->pri/dot_general | solution.py:32
  (40 shorter events, 3.4 us)
Async XLA Ops:
  7.2 91.5 %copy-start.1 = (f32[8,256]{1,0:T(8,128)S(1)}, f32[8,256]{1,0:T(8,128)}, u32[]{:S(2)}) copy-start(f32[8,256]{1,0:T(8,128)} %param.13) | copy-start | bytes 24580
  7.2 91.5 %copy-start.2 = (f32[8,256]{1,0:T(8,128)S(1)}, f32[8,256]{1,0:T(8,128)}, u32[]{:S(2)}) copy-start(f32[8,256]{1,0:T(8,128)} %param.11) | copy-start | bytes 24580
  7.2 91.5 %reduce-scatter.3.cloned.1.call-start = ((), (), s32[]{:S(2)}) async-start(), calls=%async_computation.2 | async-start | bytes 139264 | tf_op jit(solution)/shard_map/reduce_scatter | solution.py:55
  14.3 133.1 %copy-start = (f32[8,256]{1,0:T(8,128)S(1)}, f32[8,256]{1,0:T(8,128)}, u32[]{:S(2)}) copy-start(f32[8,256]{1,0:T(8,128)} %param.14) | copy-start | bytes 24580
  14.3 133.1 %copy-start.3 = (f32[8,256]{1,0:T(8,128)S(1)}, f32[8,256]{1,0:T(8,128)}, u32[]{:S(2)}) copy-start(f32[8,256]{1,0:T(8,128)} %param.12) | copy-start | bytes 24580
  15.2 3.1 %collective-permute-start = (f32[1,4096]{1,0:T(1,128)S(1)}, f32[1,4096]{1,0:T(1,128)S(1)}, u32[]{:S(2)}, u32[]{:S(2)}) collective-permute-start(f32[1,4096]{1,0:T(1,128)S(1)} %bitcast.59), channel_id=1, source_target_pairs={{16,0},{17,1},{18,2},{19,3},{20,4},{21,5},{22,6},{23,7},{24,8},{25... | collective-permute-start | bytes 49160 | tf_op jit(solution)/shard_map/ppermute | solution.py:13
  19.0 213.3 %reduce-scatter.5.cloned.1.call-start = ((), (), s32[]{:S(2)}) async-start(), calls=%async_computation.3 | async-start | bytes 139264 | tf_op jit(solution)/shard_map/reduce_scatter | solution.py:55
  136.7 2.1 collective-permute-start.1
  154.1 3.1 %collective-permute-start.2 = (f32[1,4096]{1,0:T(1,128)S(1)}, f32[1,4096]{1,0:T(1,128)S(1)}, u32[]{:S(2)}, u32[]{:S(2)}) collective-permute-start(f32[1,4096]{1,0:T(1,128)S(1)} %bitcast.60), channel_id=1, source_target_pairs={{16,0},{17,1},{18,2},{19,3},{20,4},{21,5},{22,6},{23,7},{24,8},{25... | collective-permute-start | bytes 49160 | tf_op jit(solution)/shard_map/ppermute | solution.py:13
  270.3 2.1 collective-permute-start.3
Sparse Core Ops, SparseCore 0:
  19.1 79.4 reduce-scatter.2
  158.0 74.2 reduce-scatter.4
where the time goes:
time: 289 us; the launch traced here: 288 us
  waiting for transfers between devices  119 us (41%)
  blocking collectives  110 us (38%)
  matrix products  25.4 us (9%)
  between operations  16.4 us (6%)
  other arithmetic  7.89 us (3%)
  starting transfers between devices  5.42 us (2%)
  local copies, waits for them, and re-layouts  3.43 us (1%)
    reduce_scatter x2, waiting for transfers between devices, adjoint(): result = lax.psum_scatter(merged, 'dom', scatter_dimension=1, tiled=True)  115 us
    all_gather x2, blocking collectives, forward(): gathered = lax.all_gather(field, 'dom', axis=1, tiled=True)  73.3 us
    psum x1, blocking collectives, on_device(): lax.psum((local_primal, local_dual), ('section', 'dom'))  37.2 us
    dot_general x2, matrix products, forward(): jnp.einsum('prkij,prkj->pri', blocks, picked, precision=lax.Precision.HIG...  14.2 us
    dot_general x2, matrix products, adjoint(): jnp.einsum('prkij,pri->prkj', blocks, field_blocks, precision=lax.Precisi...  11.2 us
  transfers between devices with their start and end apart: 6, of which 6 were waited for; matrix products, arithmetic and copies ran while one was open for 0% of the time, Pallas kernels for 0%

commit v1 on v0

--- a/solution.py
+++ b/solution.py
@@ -24,7 +24,14 @@
 def forward(blocks, column_index, slot_index, field):
     periods_here = field.shape[0]
     width_here = blocks.shape[-1]
-    gathered = lax.all_gather(field, "dom", axis=1, tiled=True)
+    t1, w2 = (lax.axis_size("dom"), lax.axis_index("dom"))
+    gathered, field_out = (field, 1)
+    while field_out < t1:
+        finding = lax.ppermute(gathered, "dom", [(ii, ii ^ field_out) for ii in range(t1)])
+        plain = jnp.concatenate([gathered, finding], 1)
+        upper = jnp.concatenate([finding, gathered], 1)
+        gathered = jnp.where(w2 & field_out == 0, plain, upper)
+        field_out = 2 * field_out
     carried = passed_along(gathered[-1:], "section", 1)
     stacked = jnp.concatenate([carried, gathered], axis=0)
     block_count = stacked.shape[1] // width_here

time: 289 us -> 248 us (0.86)
  blocking collectives: 110 us -> 37.9 us
  waiting for transfers between devices: 119 us -> 151 us
    all_gather x2 -> x0, blocking collectives: 73.3 us -> none  [forward(): gathered = lax.all_gather(field, 'dom', axis=1, tiled=True)]
    ppermute x0 -> x8, waiting for transfers between devices: none -> 33.2 us  [forward(): lax.ppermute(gathered, 'dom', [(ii, ii ^ field_out) for ii in range(t1)])]
  transfers between devices with their start and end apart: 6 -> 14, of which waited for: 6 -> 14; matrix products, arithmetic and copies ran while one was open for 0% -> 0% of each run, Pallas kernels for 0% -> 0%
where the time goes in v1:
time: 248 us
  waiting for transfers between devices  151 us (61%)
  blocking collectives  37.9 us (15%)
  matrix products  25.4 us (10%)
  between operations  16.5 us (7%)
  other arithmetic  7.96 us (3%)
  starting transfers between devices  5.58 us (2%)
  local copies, waits for them, and re-layouts  3.43 us (1%)
    reduce_scatter x2, waiting for transfers between devices, adjoint(): result = lax.psum_scatter(merged, 'dom', scatter_dimension=1, tiled=True)  113 us
    psum x1, blocking collectives, on_device(): lax.psum((local_primal, local_dual), ('section', 'dom'))  37.9 us
    ppermute x8, waiting for transfers between devices, forward(): lax.ppermute(gathered, 'dom', [(ii, ii ^ field_out) for ii in range(t1)])  33.2 us
    dot_general x2, matrix products, forward(): jnp.einsum('prkij,prkj->pri', blocks, picked, precision=lax.Precision.HIG...  14.2 us
    dot_general x2, matrix products, adjoint(): jnp.einsum('prkij,pri->prkj', blocks, field_blocks, precision=lax.Precisi...  11.2 us
    ppermute x4, starting transfers between devices, passed_along(): return lax.ppermute(block, axis, route)  5.35 us
  transfers between devices with their start and end apart: 14, of which 14 were waited for; matrix products, arithmetic and copies ran while one was open for 0% of the time, Pallas kernels for 0%

profile of v1, /device:TPU:0, one launch (start us, length us, event | category | flops | bytes accessed | tf_op | source)
XLA Modules:
  0.0 247.8 jit_solution(15452646120881904827)
XLA Ops:
  8.2 6.1 %fusion.10 = f32[8,2,1,6,128]{4,2,3,1,0:T(1,128)S(1)} fusion(f32[8,2,6,128,128]{4,3,2,1,0:T(8,128)} %param.8, f32[8,2,128,1,1]{2,0,1,3,4:T(8,128)} %bitcast.58), kind=kOutput, calls=%fused_computation.32 | convolution fusion | flops 18874368 | bytes 6348800 | tf_op jit(solution)/shard_map/prkij,pri->prkj/dot_general | solution.py:49
  15.3 1.3 collective-permute-start
  16.6 1.7 collective-permute-done
  19.8 78.9 %reduce-scatter.3.cloned.1.call-done = f32[8,256]{1,0:T(8,128)} async-done(((f32[8,4096]{1,0:T(8,128)}), f32[8,256]{1,0:T(8,128)}) %reduce-scatter.3.cloned.1.call-update) | async-done | bytes 8208 | tf_op jit(solution)/shard_map/reduce_scatter | solution.py:62
  98.7 1.3 multiply_reduce_fusion
  100.0 3.6 %collective-permute-done.1 = f32[8,256]{1,0:T(8,128)S(1)} collective-permute-done((f32[8,256]{1,0:T(8,128)S(1)}, f32[8,256]{1,0:T(8,128)S(1)}, u32[]{:S(2)}, u32[]{:S(2)}) %collective-permute-start.1) | collective-permute-done | bytes 8224 | tf_op jit(solution)/shard_map/ppermute | solution.py:30
  103.7 3.7 %collective-permute-done.2 = f32[8,512]{1,0:T(8,128)S(1)} collective-permute-done((f32[8,512]{1,0:T(8,128)S(1)}, f32[8,512]{1,0:T(8,128)S(1)}, u32[]{:S(2)}, u32[]{:S(2)}) %collective-permute-start.2) | collective-permute-done | bytes 16416 | tf_op jit(solution)/shard_map/ppermute | solution.py:30
  107.4 3.9 %collective-permute-done.3 = f32[8,1024]{1,0:T(8,128)S(1)} collective-permute-done((f32[8,1024]{1,0:T(8,128)S(1)}, f32[8,1024]{1,0:T(8,128)S(1)}, u32[]{:S(2)}, u32[]{:S(2)}) %collective-permute-start.3) | collective-permute-done | bytes 32800 | tf_op jit(solution)/shard_map/ppermute | solution.py:30
  111.4 5.3 %collective-permute-done.4 = f32[8,2048]{1,0:T(8,128)S(1)} collective-permute-done((f32[8,2048]{1,0:T(8,128)S(1)}, f32[8,2048]{1,0:T(8,128)S(1)}, u32[]{:S(2)}, u32[]{:S(2)}) %collective-permute-start.4) | collective-permute-done | bytes 65568 | tf_op jit(solution)/shard_map/ppermute | solution.py:30
  119.0 1.4 gather_fusion
  120.4 7.1 %fusion.18 = f32[8,2,1,128,1]{3,2,4,1,0:T(1,128)S(1)} fusion(f32[8,2,6,128,1]{3,4,2,1,0:T(1,128)S(1)} %bitcast.54, f32[8,2,6,128,128]{4,3,2,1,0:T(8,128)} %param.8), kind=kOutput, calls=%fused_computation.48 | convolution fusion | flops 18874368 | bytes 6348800 | tf_op jit(solution)/shard_map/prkij,prkj->pri/dot_general | solution.py:39
  128.1 5.1 %fusion.8 = f32[8,2,1,6,128]{4,2,3,1,0:T(1,128)S(1)} fusion(f32[8,2,6,128,128]{4,3,2,1,0:T(8,128)} %param.8, f32[8,2,128,1,1]{2,0,1,3,4:T(8,128)S(1)} %bitcast.57), kind=kOutput, calls=%fused_computation.30 | convolution fusion | flops 18874368 | bytes 6348800 | tf_op jit(solution)/shard_map/prkij,pri->prkj/dot_general | solution.py:49
  134.2 1.3 collective-permute-start.6
  135.5 1.7 collective-permute-done.6
  138.0 37.9 %all-reduce.2 = (f32[]{:T(128)}, f32[]{:T(128)}) all-reduce(f32[]{:T(128)} %get-tuple-element.8, f32[]{:T(128)} %get-tuple-element.6), channel_id=1, replica_groups=mesh['section'=2,'dom'=16] {'section','dom'}, use_global_device_ids=true, to_apply=%region_3.4 | all-reduce | flops 2 | bytes 16 | tf_op jit(solution)/shard_map/psum | solution.py:83
  177.3 34.3 %reduce-scatter.5.cloned.1.call-done = f32[8,256]{1,0:T(8,128)} async-done(((f32[8,4096]{1,0:T(8,128)}), f32[8,256]{1,0:T(8,128)}) %reduce-scatter.5.cloned.1.call-update) | async-done | bytes 8208 | tf_op jit(solution)/shard_map/reduce_scatter | solution.py:62
  211.6 1.3 multiply_subtract_fusion
  212.9 3.6 %collective-permute-done.7 = f32[8,256]{1,0:T(8,128)S(1)} collective-permute-done((f32[8,256]{1,0:T(8,128)S(1)}, f32[8,256]{1,0:T(8,128)S(1)}, u32[]{:S(2)}, u32[]{:S(2)}) %collective-permute-start.7) | collective-permute-done | bytes 8224 | tf_op jit(solution)/shard_map/ppermute | solution.py:30
  216.6 3.7 %collective-permute-done.8 = f32[8,512]{1,0:T(8,128)S(1)} collective-permute-done((f32[8,512]{1,0:T(8,128)S(1)}, f32[8,512]{1,0:T(8,128)S(1)}, u32[]{:S(2)}, u32[]{:S(2)}) %collective-permute-start.8) | collective-permute-done | bytes 16416 | tf_op jit(solution)/shard_map/ppermute | solution.py:30
  220.3 3.9 %collective-permute-done.9 = f32[8,1024]{1,0:T(8,128)S(1)} collective-permute-done((f32[8,1024]{1,0:T(8,128)S(1)}, f32[8,1024]{1,0:T(8,128)S(1)}, u32[]{:S(2)}, u32[]{:S(2)}) %collective-permute-start.9) | collective-permute-done | bytes 32800 | tf_op jit(solution)/shard_map/ppermute | solution.py:30
  224.3 5.3 %collective-permute-done.10 = f32[8,2048]{1,0:T(8,128)S(1)} collective-permute-done((f32[8,2048]{1,0:T(8,128)S(1)}, f32[8,2048]{1,0:T(8,128)S(1)}, u32[]{:S(2)}, u32[]{:S(2)}) %collective-permute-start.10) | collective-permute-done | bytes 65568 | tf_op jit(solution)/shard_map/ppermute | solution.py:30
  229.6 1.5 collective-permute-start.11
  231.9 1.4 gather_fusion.1
  233.3 7.1 %fusion.19 = f32[8,2,1,128,1]{3,2,4,1,0:T(1,128)S(1)} fusion(f32[8,2,6,128,1]{3,4,2,1,0:T(1,128)S(1)} %bitcast.53, f32[8,2,6,128,128]{4,3,2,1,0:T(8,128)} %param.8), kind=kOutput, calls=%fused_computation.49 | convolution fusion | flops 18874368 | bytes 6348800 | tf_op jit(solution)/shard_map/prkij,prkj->pri/dot_general | solution.py:39
  (62 shorter events, 8.8 us)
Async XLA Ops:
  7.2 91.5 %copy-start.1 = (f32[8,256]{1,0:T(8,128)S(1)}, f32[8,256]{1,0:T(8,128)}, u32[]{:S(2)}) copy-start(f32[8,256]{1,0:T(8,128)} %param.13) | copy-start | bytes 24580
  7.2 91.5 %copy-start.2 = (f32[8,256]{1,0:T(8,128)S(1)}, f32[8,256]{1,0:T(8,128)}, u32[]{:S(2)}) copy-start(f32[8,256]{1,0:T(8,128)} %param.11) | copy-start | bytes 24580
  7.2 91.5 %reduce-scatter.3.cloned.1.call-start = ((), (), s32[]{:S(2)}) async-start(), calls=%async_computation.2 | async-start | bytes 139264 | tf_op jit(solution)/shard_map/reduce_scatter | solution.py:62
  14.3 113.2 %copy-start = (f32[8,256]{1,0:T(8,128)S(1)}, f32[8,256]{1,0:T(8,128)}, u32[]{:S(2)}) copy-start(f32[8,256]{1,0:T(8,128)} %param.14) | copy-start | bytes 24580
  14.3 113.2 %copy-start.3 = (f32[8,256]{1,0:T(8,128)S(1)}, f32[8,256]{1,0:T(8,128)}, u32[]{:S(2)}) copy-start(f32[8,256]{1,0:T(8,128)} %param.12) | copy-start | bytes 24580
  15.3 3.1 %collective-permute-start = (f32[1,4096]{1,0:T(1,128)S(1)}, f32[1,4096]{1,0:T(1,128)S(1)}, u32[]{:S(2)}, u32[]{:S(2)}) collective-permute-start(f32[1,4096]{1,0:T(1,128)S(1)} %bitcast.59), channel_id=1, source_target_pairs={{16,0},{17,1},{18,2},{19,3},{20,4},{21,5},{22,6},{23,7},{24,8},{25... | collective-permute-start | bytes 49160 | tf_op jit(solution)/shard_map/ppermute | solution.py:13
  19.0 192.6 %reduce-scatter.5.cloned.1.call-start = ((), (), s32[]{:S(2)}) async-start(), calls=%async_computation.3 | async-start | bytes 139264 | tf_op jit(solution)/shard_map/reduce_scatter | solution.py:62
  100.0 3.7 %collective-permute-start.1 = (f32[8,256]{1,0:T(8,128)S(1)}, f32[8,256]{1,0:T(8,128)S(1)}, u32[]{:S(2)}, u32[]{:S(2)}) collective-permute-start(f32[8,256]{1,0:T(8,128)S(1)} %multiply_subtract_fusion.1), channel_id=1, source_target_pairs={{0,1},{1,0},{2,3},{3,2},{4,5},{5,4},{6,7},{7,6},{8,9},{9,8},{10,11... | collective-permute-start | bytes 24584 | tf_op jit(solution)/shard_map/ppermute | solution.py:30
  103.7 3.7 %collective-permute-start.2 = (f32[8,512]{1,0:T(8,128)S(1)}, f32[8,512]{1,0:T(8,128)S(1)}, u32[]{:S(2)}, u32[]{:S(2)}) collective-permute-start(f32[8,512]{1,0:T(8,128)S(1)} %maximum_select_fusion.6), channel_id=1, source_target_pairs={{0,2},{1,3},{2,0},{3,1},{4,6},{5,7},{6,4},{7,5},{8,10},{9,11},{10,... | collective-permute-start | bytes 49160 | tf_op jit(solution)/shard_map/ppermute | solution.py:30
  107.4 3.9 %collective-permute-start.3 = (f32[8,1024]{1,0:T(8,128)S(1)}, f32[8,1024]{1,0:T(8,128)S(1)}, u32[]{:S(2)}, u32[]{:S(2)}) collective-permute-start(f32[8,1024]{1,0:T(8,128)S(1)} %maximum_select_fusion.4), channel_id=1, source_target_pairs={{0,4},{1,5},{2,6},{3,7},{4,0},{5,1},{6,2},{7,3},{8,12},{9,13},{10,... | collective-permute-start | bytes 98312 | tf_op jit(solution)/shard_map/ppermute | solution.py:30
  111.3 5.4 %collective-permute-start.4 = (f32[8,2048]{1,0:T(8,128)S(1)}, f32[8,2048]{1,0:T(8,128)S(1)}, u32[]{:S(2)}, u32[]{:S(2)}) collective-permute-start(f32[8,2048]{1,0:T(8,128)S(1)} %maximum_select_fusion.2), channel_id=1, source_target_pairs={{0,8},{1,9},{2,10},{3,11},{4,12},{5,13},{6,14},{7,15},{8,0},{9,1},... | collective-permute-start | bytes 196616 | tf_op jit(solution)/shard_map/ppermute | solution.py:30
  116.7 2.1 collective-permute-start.5
  134.2 3.1 %collective-permute-start.6 = (f32[1,4096]{1,0:T(1,128)S(1)}, f32[1,4096]{1,0:T(1,128)S(1)}, u32[]{:S(2)}, u32[]{:S(2)}) collective-permute-start(f32[1,4096]{1,0:T(1,128)S(1)} %bitcast.60), channel_id=1, source_target_pairs={{16,0},{17,1},{18,2},{19,3},{20,4},{21,5},{22,6},{23,7},{24,8},{25... | collective-permute-start | bytes 49160 | tf_op jit(solution)/shard_map/ppermute | solution.py:13
  212.9 3.7 %collective-permute-start.7 = (f32[8,256]{1,0:T(8,128)S(1)}, f32[8,256]{1,0:T(8,128)S(1)}, u32[]{:S(2)}, u32[]{:S(2)}) collective-permute-start(f32[8,256]{1,0:T(8,128)S(1)} %get-tuple-element.4), channel_id=1, source_target_pairs={{0,1},{1,0},{2,3},{3,2},{4,5},{5,4},{6,7},{7,6},{8,9},{9,8},{10,11... | collective-permute-start | bytes 24584 | tf_op jit(solution)/shard_map/ppermute | solution.py:30
  216.6 3.7 %collective-permute-start.8 = (f32[8,512]{1,0:T(8,128)S(1)}, f32[8,512]{1,0:T(8,128)S(1)}, u32[]{:S(2)}, u32[]{:S(2)}) collective-permute-start(f32[8,512]{1,0:T(8,128)S(1)} %maximum_select_fusion.7), channel_id=1, source_target_pairs={{0,2},{1,3},{2,0},{3,1},{4,6},{5,7},{6,4},{7,5},{8,10},{9,11},{10,... | collective-permute-start | bytes 49160 | tf_op jit(solution)/shard_map/ppermute | solution.py:30
  220.3 3.9 %collective-permute-start.9 = (f32[8,1024]{1,0:T(8,128)S(1)}, f32[8,1024]{1,0:T(8,128)S(1)}, u32[]{:S(2)}, u32[]{:S(2)}) collective-permute-start(f32[8,1024]{1,0:T(8,128)S(1)} %maximum_select_fusion.5), channel_id=1, source_target_pairs={{0,4},{1,5},{2,6},{3,7},{4,0},{5,1},{6,2},{7,3},{8,12},{9,13},{10,... | collective-permute-start | bytes 98312 | tf_op jit(solution)/shard_map/ppermute | solution.py:30
  224.2 5.4 %collective-permute-start.10 = (f32[8,2048]{1,0:T(8,128)S(1)}, f32[8,2048]{1,0:T(8,128)S(1)}, u32[]{:S(2)}, u32[]{:S(2)}) collective-permute-start(f32[8,2048]{1,0:T(8,128)S(1)} %maximum_select_fusion.3), channel_id=1, source_target_pairs={{0,8},{1,9},{2,10},{3,11},{4,12},{5,13},{6,14},{7,15},{8,0},{9,1},... | collective-permute-start | bytes 196616 | tf_op jit(solution)/shard_map/ppermute | solution.py:30
  229.6 2.1 collective-permute-start.11
Sparse Core Ops, SparseCore 0:
  19.1 79.4 reduce-scatter.2
  138.1 73.4 reduce-scatter.4
